TPU v7x, 32 devices: a whole 2x2x4 slice. The times are simulated.
32 devices in a mesh: pipe: 2 (over y), ctx: 16 (over z, x, core).
Axes of the slice: x: 2, y: 2, z: 4, core: 2. Of those that a mesh axis runs over, the one named last changes fastest.
Arguments:
- saved_qkv: bfloat16 [2, 3, 2048, 2048], P('pipe', None, 'ctx'), may hold values from -6 to 6
- handed: bfloat16 [2, 2048, 2048], P('pipe', 'ctx'), may hold values from -6 to 6
- long_filter: bfloat16 [2, 128, 128], P('pipe'), may hold values from -0.5 to 0.5
- short_filter: bfloat16 [2, 3, 3, 2048], P('pipe'), may hold values from -3.5 to 3.5
- doc_lengths: int32 [16], replicated, may hold values from 1 to 512, 2048 in all
Outputs:
- grad_pre: bfloat16 [2, 3, 2048, 2048], P('pipe', None, 'ctx')
- filter_grad: float32 [2, 128, 128], P('pipe')
Inputs may be any that keep to these rules, and one draw needn't show every extreme that they name: `doc_lengths`: documents lie end to end and sum to 2048 tokens; the longest has exactly 512 tokens.
All inputs are finite; a program needn't handle non-finite values.
Results may differ from a plain program's by a relative error of at most 0.0058.
Values may be sent and summed in bfloat16 or wider, within the bound.
A program may use at most 64 MiB of HBM per device.

v0:
```python
import math
import jax
import jax.numpy as jnp
from jax import lax
from jax.sharding import PartitionSpec as P


def from_behind(shard, axis, by):
    count = lax.axis_size(axis)
    return lax.ppermute(shard, axis, [(i, (i + by) % count) for i in range(count)])


def shifted_2(block, axis, distance):
    devices = range(lax.axis_size(axis))
    route = [(i - distance, i) for i in devices if i - distance in devices]
    return lax.ppermute(block, axis, route)


def back_conv(grad_rows, grad_pos, filt, out_len, members, unroll):
    tap_count = filt.shape[0]
    channels = grad_rows.shape[1]

    def step(total, base):
        for offset in range(unroll):
            lag = base * unroll + offset
            ahead = lax.dynamic_slice_in_dim(grad_rows, lag, out_len, 0).astype(jnp.float32)
            ahead_pos = lax.dynamic_slice_in_dim(grad_pos, lag, out_len, 0)
            weights = jnp.repeat(filt[lag].astype(jnp.float32), members)
            total = total + jnp.where((lag <= ahead_pos)[:, None], ahead * weights[None, :], 0.0)
        return (total, None)

    bases = jnp.arange(tap_count // unroll, dtype=jnp.int32)
    result, _ = lax.scan(step, jnp.zeros((out_len, channels), jnp.float32), bases)
    return result


def body(saved_qkv, handed, long_filter, short_filter, doc_lengths):
    query_rows = saved_qkv[0, 0]
    key_rows = saved_qkv[0, 1]
    value_rows = saved_qkv[0, 2]
    filt = long_filter[0]
    tap_count, groups = filt.shape
    row_count, channels = query_rows.shape
    members = channels // groups
    short_taps = short_filter.shape[2]
    unroll = math.gcd(tap_count, 16)
    devices = lax.axis_size("ctx")
    device_index = lax.axis_index("ctx")
    starts = jnp.cumsum(doc_lengths) - doc_lengths
    global_rows = device_index * row_count + jnp.arange(row_count + tap_count, dtype=jnp.int32)
    latest = jnp.max(jnp.where(starts[None, :] <= global_rows[:, None], starts[None, :], 0), axis=1)
    position = global_rows - latest
    own_pos = position[:row_count]
    incoming = from_behind(handed[0], "pipe", -1)
    product = (key_rows.astype(jnp.float32) * value_rows.astype(jnp.float32)).astype(jnp.bfloat16)
    tail_rows = shifted_2(product, "ctx", 1)
    extended = jnp.concatenate([tail_rows, product], axis=0)
    conv_grad = (incoming.astype(jnp.float32) * query_rows.astype(jnp.float32)).astype(jnp.bfloat16)
    grad_wide = conv_grad.astype(jnp.float32)

    def forward_step(total, base):
        columns = []
        for offset in range(unroll):
            lag = base * unroll + offset
            shifted = lax.dynamic_slice_in_dim(extended, tap_count - lag, row_count, 0).astype(
                jnp.float32
            )
            weights = jnp.repeat(filt[lag].astype(jnp.float32), members)
            usable = (lag <= own_pos)[:, None]
            total = total + jnp.where(usable, shifted * weights[None, :], 0.0)
            pair = jnp.sum(
                (grad_wide * shifted).reshape(row_count, groups, members), axis=2
            ).astype(jnp.bfloat16)
            pair = lax.optimization_barrier(pair).astype(jnp.float32)
            columns.append(jnp.sum(jnp.where(usable, pair, 0.0), axis=0))
        return (total, jnp.stack(columns))

    bases = jnp.arange(tap_count // unroll, dtype=jnp.int32)
    conv_out, filter_cols = lax.scan(
        forward_step, jnp.zeros((row_count, channels), jnp.float32), bases
    )
    filter_sum = filter_cols.reshape(tap_count, groups)
    head_rows = shifted_2(conv_grad, "ctx", -1)
    joined = jnp.concatenate([conv_grad, head_rows], axis=0)
    own_grad = back_conv(joined, position, filt, row_count, members, unroll)
    query_grad = (incoming.astype(jnp.float32) * conv_out).astype(jnp.bfloat16)
    key_grad = (own_grad * value_rows.astype(jnp.float32)).astype(jnp.bfloat16)
    value_grad = (own_grad * key_rows.astype(jnp.float32)).astype(jnp.bfloat16)
    stacked = jnp.stack([query_grad, key_grad, value_grad])
    rim_rows = shifted_2(stacked[:, : short_taps - 1], "ctx", -1)
    stacked_ext = jnp.concatenate([stacked, rim_rows], axis=1)
    weights_all = short_filter[0]
    total = jnp.zeros((3, row_count, channels), jnp.float32)
    for shift_by in range(short_taps):
        usable = (shift_by <= position[shift_by : shift_by + row_count])[None, :, None]
        weights = weights_all[:, shift_by].astype(jnp.float32)[:, None, :]
        total = total + jnp.where(
            usable,
            weights * stacked_ext[:, shift_by : shift_by + row_count].astype(jnp.float32),
            0.0,
        )
    grad_pre = total.astype(jnp.bfloat16)[None]
    summed = lax.psum(filter_sum, "ctx")
    filter_grad = (summed / math.sqrt(row_count * devices * members))[None]
    return (grad_pre, filter_grad)


def solution(mesh):
    return jax.shard_map(
        body,
        mesh=mesh,
        in_specs=(
            P("pipe", None, "ctx", None),
            P("pipe", "ctx", None),
            P("pipe", None, None),
            P("pipe", None, None, None),
            P(),
        ),
        out_specs=(P("pipe", None, "ctx", None), P("pipe", None, None)),
        check_vma=False,
    )
```

profile of v0, /device:TPU:8, one launch (start us, length us, event | category | flops | bytes accessed | tf_op | source)
XLA Modules:
  0.0 410.6 jit_solution(385893030262521515)
XLA Ops:
  7.2 1.6 collective-permute-start
  8.8 12.4 %collective-permute-done = bf16[128,2048]{1,0:T(8,128)(2,1)S(1)} collective-permute-done((bf16[128,2048]{1,0:T(8,128)(2,1)}, bf16[128,2048]{1,0:T(8,128)(2,1)S(1)}, u32[]{:S(2)}, u32[]{:S(2)}) %collective-permute-start) | collective-permute-done | bytes 524320 | tf_op jit(solution)/shard_map/ppermute | solution.py:10
  21.2 1.4 fusion.112
  22.6 1.9 collective-permute-start.2
  24.5 0.7 copy.16
  26.2 5.0 %collective-permute-done.2 = bf16[128,2048]{1,0:T(8,128)(2,1)S(1)} collective-permute-done((bf16[128,2048]{1,0:T(8,128)(2,1)S(1)}, bf16[128,2048]{1,0:T(8,128)(2,1)S(1)}, u32[]{:S(2)}, u32[]{:S(2)}) %collective-permute-start.2) | collective-permute-done | bytes 524320 | tf_op jit(solution)/shard_map/ppermute | solution.py:16
  31.3 81.4 %while.30 = (s32[]{:T(128)}, f32[128,2048]{1,0:T(8,128)S(1)}, s32[8]{0:T(128)S(1)}, s32[256]{0:T(256)S(1)}, bf16[256,2048]{1,0:T(8,128)(2,1)S(1)}, /*index=5*/bf...) while((s32[]{:T(128)}, f32[128,2048]{1,0:T(8,128)S(1)}, ...), condition=%wide.region_37.38_spmd.clone, body=%wide.region_36.37_spmd.clone.sunk | while | flops 17043556 | bytes 11044691 | solution.py:33
  31.3 0.7 dynamic_slice.941
  35.9 5.6 %fusion.128 = f32[128,2048]{1,0:T(8,128)S(1)} fusion(f32[128,2048]{1,0:T(8,128)S(1)} %get-tuple-element.835, f32[2048]{0:T(1024)S(1)} %mul.1435, bf16[256,2048]{1,0:T(8,128)(2,1)S(1)} %get-tuple-element.893, s32[]{:T(128)S(6)} %select_n.1196, f32[2048]{0:T(1024)S(1)} %mul.1436, s32[]{:T(128)S(6)} %select_n.1197, f32[2048]{0:T(1024)S(1)} %mul.1437, ...), kind=kLoop, calls=%fused_computation.176.clone.1 | loop fusion | flops 17039360 | bytes 10618945 | tf_op jit(solution)/shard_map/while/body/eval_jaxpr/add | solution.py:29
  41.5 0.7 dynamic_slice.941
  46.1 5.6 %fusion.128 = f32[128,2048]{1,0:T(8,128)S(1)} fusion(f32[128,2048]{1,0:T(8,128)S(1)} %get-tuple-element.835, f32[2048]{0:T(1024)S(1)} %mul.1435, bf16[256,2048]{1,0:T(8,128)(2,1)S(1)} %get-tuple-element.893, s32[]{:T(128)S(6)} %select_n.1196, f32[2048]{0:T(1024)S(1)} %mul.1436, s32[]{:T(128)S(6)} %select_n.1197, f32[2048]{0:T(1024)S(1)} %mul.1437, ...), kind=kLoop, calls=%fused_computation.176.clone.1 | loop fusion | flops 17039360 | bytes 10618945 | tf_op jit(solution)/shard_map/while/body/eval_jaxpr/add | solution.py:29
  51.7 0.7 dynamic_slice.941
  56.2 5.6 %fusion.128 = f32[128,2048]{1,0:T(8,128)S(1)} fusion(f32[128,2048]{1,0:T(8,128)S(1)} %get-tuple-element.835, f32[2048]{0:T(1024)S(1)} %mul.1435, bf16[256,2048]{1,0:T(8,128)(2,1)S(1)} %get-tuple-element.893, s32[]{:T(128)S(6)} %select_n.1196, f32[2048]{0:T(1024)S(1)} %mul.1436, s32[]{:T(128)S(6)} %select_n.1197, f32[2048]{0:T(1024)S(1)} %mul.1437, ...), kind=kLoop, calls=%fused_computation.176.clone.1 | loop fusion | flops 17039360 | bytes 10618945 | tf_op jit(solution)/shard_map/while/body/eval_jaxpr/add | solution.py:29
  61.9 0.7 dynamic_slice.941
  66.4 5.6 %fusion.128 = f32[128,2048]{1,0:T(8,128)S(1)} fusion(f32[128,2048]{1,0:T(8,128)S(1)} %get-tuple-element.835, f32[2048]{0:T(1024)S(1)} %mul.1435, bf16[256,2048]{1,0:T(8,128)(2,1)S(1)} %get-tuple-element.893, s32[]{:T(128)S(6)} %select_n.1196, f32[2048]{0:T(1024)S(1)} %mul.1436, s32[]{:T(128)S(6)} %select_n.1197, f32[2048]{0:T(1024)S(1)} %mul.1437, ...), kind=kLoop, calls=%fused_computation.176.clone.1 | loop fusion | flops 17039360 | bytes 10618945 | tf_op jit(solution)/shard_map/while/body/eval_jaxpr/add | solution.py:29
  72.0 0.7 dynamic_slice.941
  76.6 5.6 %fusion.128 = f32[128,2048]{1,0:T(8,128)S(1)} fusion(f32[128,2048]{1,0:T(8,128)S(1)} %get-tuple-element.835, f32[2048]{0:T(1024)S(1)} %mul.1435, bf16[256,2048]{1,0:T(8,128)(2,1)S(1)} %get-tuple-element.893, s32[]{:T(128)S(6)} %select_n.1196, f32[2048]{0:T(1024)S(1)} %mul.1436, s32[]{:T(128)S(6)} %select_n.1197, f32[2048]{0:T(1024)S(1)} %mul.1437, ...), kind=kLoop, calls=%fused_computation.176.clone.1 | loop fusion | flops 17039360 | bytes 10618945 | tf_op jit(solution)/shard_map/while/body/eval_jaxpr/add | solution.py:29
  86.7 5.6 %fusion.128 = f32[128,2048]{1,0:T(8,128)S(1)} fusion(f32[128,2048]{1,0:T(8,128)S(1)} %get-tuple-element.835, f32[2048]{0:T(1024)S(1)} %mul.1435, bf16[256,2048]{1,0:T(8,128)(2,1)S(1)} %get-tuple-element.893, s32[]{:T(128)S(6)} %select_n.1196, f32[2048]{0:T(1024)S(1)} %mul.1436, s32[]{:T(128)S(6)} %select_n.1197, f32[2048]{0:T(1024)S(1)} %mul.1437, ...), kind=kLoop, calls=%fused_computation.176.clone.1 | loop fusion | flops 17039360 | bytes 10618945 | tf_op jit(solution)/shard_map/while/body/eval_jaxpr/add | solution.py:29
  96.9 5.6 %fusion.128 = f32[128,2048]{1,0:T(8,128)S(1)} fusion(f32[128,2048]{1,0:T(8,128)S(1)} %get-tuple-element.835, f32[2048]{0:T(1024)S(1)} %mul.1435, bf16[256,2048]{1,0:T(8,128)(2,1)S(1)} %get-tuple-element.893, s32[]{:T(128)S(6)} %select_n.1196, f32[2048]{0:T(1024)S(1)} %mul.1436, s32[]{:T(128)S(6)} %select_n.1197, f32[2048]{0:T(1024)S(1)} %mul.1437, ...), kind=kLoop, calls=%fused_computation.176.clone.1 | loop fusion | flops 17039360 | bytes 10618945 | tf_op jit(solution)/shard_map/while/body/eval_jaxpr/add | solution.py:29
  107.1 5.6 %fusion.128 = f32[128,2048]{1,0:T(8,128)S(1)} fusion(f32[128,2048]{1,0:T(8,128)S(1)} %get-tuple-element.835, f32[2048]{0:T(1024)S(1)} %mul.1435, bf16[256,2048]{1,0:T(8,128)(2,1)S(1)} %get-tuple-element.893, s32[]{:T(128)S(6)} %select_n.1196, f32[2048]{0:T(1024)S(1)} %mul.1436, s32[]{:T(128)S(6)} %select_n.1197, f32[2048]{0:T(1024)S(1)} %mul.1437, ...), kind=kLoop, calls=%fused_computation.176.clone.1 | loop fusion | flops 17039360 | bytes 10618945 | tf_op jit(solution)/shard_map/while/body/eval_jaxpr/add | solution.py:29
  112.7 2.6 fusion.118
  115.3 3.8 collective-permute-start.1
  119.5 7.5 %collective-permute-done.1 = bf16[128,2048]{1,0:T(8,128)(2,1)} collective-permute-done((bf16[128,2048]{1,0:T(8,128)(2,1)S(1)}, bf16[128,2048]{1,0:T(8,128)(2,1)}, u32[]{:S(2)}, u32[]{:S(2)}) %collective-permute-start.1) | collective-permute-done | bytes 524320 | tf_op jit(solution)/shard_map/ppermute | solution.py:16
  127.0 2.2 pad_maximum_fusion.2
  129.1 1.5 copy.17
  130.6 178.6 %while.29 = (s32[]{:T(128)}, f32[128,2048]{0,1:T(8,128)S(1)}, f32[8,16,128]{2,1,0:T(8,128)}, s32[8]{0:T(128)S(1)}, s32[128]{0:T(128)S(1)}, /*index=5*/bf16[256,2...) while((s32[]{:T(128)}, f32[128,2048]{0,1:T(8,128)S(1)}, ...), condition=%wide.region_35.36_spmd.clone, body=%wide.region_2.35_spmd.clone.sunk | while | flops 30148740 | bytes 21566524 | solution.py:79
  132.0 6.9 %bitcast_reduce_fusion.17 = (bf16[128,128]{0,1:T(8,128)(2,1)S(1)}, bf16[128,128]{0,1:T(8,128)(2,1)S(1)}, bf16[128,128]{0,1:T(8,128)(2,1)S(1)}, bf16[128,128]{0,1...) fusion(f32[128,2048]{0,1:T(8,128)S(1)} %get-tuple-element.1035,, ...), kind=kLoop, calls=%fused_computation.64.clone.1 | loop fusion | flops 12320768 | bytes 9961536 | tf_op jit(solution)/shard_map/while/body/eval_jaxpr/reduce_sum | solution.py:71
  143.3 9.6 %fusion.126 = f32[128,2048]{0,1:T(8,128)S(1)} fusion(f32[128,2048]{0,1:T(8,128)S(1)} %get-tuple-element.987, f32[2048]{0:T(1024)S(1)} %mul.1386, f32[2048]{0:T(1024)S(1)} %mul.1387, f32[2048]{0:T(1024)S(1)} %mul.1388, f32[2048]{0:T(1024)S(1)} %mul.1389, f32[2048]{0:T(1024)S(1)} %mul.1390, f32[2048]{0:T(1024)S(1)} %mul.1391, f32[2048]{0:T(1024)S(1)} %mul.1392, ...), kind=kLoop, calls=%fused_computation.48.clone.1 | loop fusion | flops 17039360 | bytes 10618945 | tf_op jit(solution)/shard_map/while/body/eval_jaxpr/add | solution.py:70
  154.3 6.9 %bitcast_reduce_fusion.17 = (bf16[128,128]{0,1:T(8,128)(2,1)S(1)}, bf16[128,128]{0,1:T(8,128)(2,1)S(1)}, bf16[128,128]{0,1:T(8,128)(2,1)S(1)}, bf16[128,128]{0,1...) fusion(f32[128,2048]{0,1:T(8,128)S(1)} %get-tuple-element.1035,, ...), kind=kLoop, calls=%fused_computation.64.clone.1 | loop fusion | flops 12320768 | bytes 9961536 | tf_op jit(solution)/shard_map/while/body/eval_jaxpr/reduce_sum | solution.py:71
  165.7 9.6 %fusion.126 = f32[128,2048]{0,1:T(8,128)S(1)} fusion(f32[128,2048]{0,1:T(8,128)S(1)} %get-tuple-element.987, f32[2048]{0:T(1024)S(1)} %mul.1386, f32[2048]{0:T(1024)S(1)} %mul.1387, f32[2048]{0:T(1024)S(1)} %mul.1388, f32[2048]{0:T(1024)S(1)} %mul.1389, f32[2048]{0:T(1024)S(1)} %mul.1390, f32[2048]{0:T(1024)S(1)} %mul.1391, f32[2048]{0:T(1024)S(1)} %mul.1392, ...), kind=kLoop, calls=%fused_computation.48.clone.1 | loop fusion | flops 17039360 | bytes 10618945 | tf_op jit(solution)/shard_map/while/body/eval_jaxpr/add | solution.py:70
  176.7 6.9 %bitcast_reduce_fusion.17 = (bf16[128,128]{0,1:T(8,128)(2,1)S(1)}, bf16[128,128]{0,1:T(8,128)(2,1)S(1)}, bf16[128,128]{0,1:T(8,128)(2,1)S(1)}, bf16[128,128]{0,1...) fusion(f32[128,2048]{0,1:T(8,128)S(1)} %get-tuple-element.1035,, ...), kind=kLoop, calls=%fused_computation.64.clone.1 | loop fusion | flops 12320768 | bytes 9961536 | tf_op jit(solution)/shard_map/while/body/eval_jaxpr/reduce_sum | solution.py:71
  188.0 9.6 %fusion.126 = f32[128,2048]{0,1:T(8,128)S(1)} fusion(f32[128,2048]{0,1:T(8,128)S(1)} %get-tuple-element.987, f32[2048]{0:T(1024)S(1)} %mul.1386, f32[2048]{0:T(1024)S(1)} %mul.1387, f32[2048]{0:T(1024)S(1)} %mul.1388, f32[2048]{0:T(1024)S(1)} %mul.1389, f32[2048]{0:T(1024)S(1)} %mul.1390, f32[2048]{0:T(1024)S(1)} %mul.1391, f32[2048]{0:T(1024)S(1)} %mul.1392, ...), kind=kLoop, calls=%fused_computation.48.clone.1 | loop fusion | flops 17039360 | bytes 10618945 | tf_op jit(solution)/shard_map/while/body/eval_jaxpr/add | solution.py:70
  199.0 6.9 %bitcast_reduce_fusion.17 = (bf16[128,128]{0,1:T(8,128)(2,1)S(1)}, bf16[128,128]{0,1:T(8,128)(2,1)S(1)}, bf16[128,128]{0,1:T(8,128)(2,1)S(1)}, bf16[128,128]{0,1...) fusion(f32[128,2048]{0,1:T(8,128)S(1)} %get-tuple-element.1035,, ...), kind=kLoop, calls=%fused_computation.64.clone.1 | loop fusion | flops 12320768 | bytes 9961536 | tf_op jit(solution)/shard_map/while/body/eval_jaxpr/reduce_sum | solution.py:71
  210.3 9.6 %fusion.126 = f32[128,2048]{0,1:T(8,128)S(1)} fusion(f32[128,2048]{0,1:T(8,128)S(1)} %get-tuple-element.987, f32[2048]{0:T(1024)S(1)} %mul.1386, f32[2048]{0:T(1024)S(1)} %mul.1387, f32[2048]{0:T(1024)S(1)} %mul.1388, f32[2048]{0:T(1024)S(1)} %mul.1389, f32[2048]{0:T(1024)S(1)} %mul.1390, f32[2048]{0:T(1024)S(1)} %mul.1391, f32[2048]{0:T(1024)S(1)} %mul.1392, ...), kind=kLoop, calls=%fused_computation.48.clone.1 | loop fusion | flops 17039360 | bytes 10618945 | tf_op jit(solution)/shard_map/while/body/eval_jaxpr/add | solution.py:70
  221.3 6.9 %bitcast_reduce_fusion.17 = (bf16[128,128]{0,1:T(8,128)(2,1)S(1)}, bf16[128,128]{0,1:T(8,128)(2,1)S(1)}, bf16[128,128]{0,1:T(8,128)(2,1)S(1)}, bf16[128,128]{0,1...) fusion(f32[128,2048]{0,1:T(8,128)S(1)} %get-tuple-element.1035,, ...), kind=kLoop, calls=%fused_computation.64.clone.1 | loop fusion | flops 12320768 | bytes 9961536 | tf_op jit(solution)/shard_map/while/body/eval_jaxpr/reduce_sum | solution.py:71
  232.7 9.6 %fusion.126 = f32[128,2048]{0,1:T(8,128)S(1)} fusion(f32[128,2048]{0,1:T(8,128)S(1)} %get-tuple-element.987, f32[2048]{0:T(1024)S(1)} %mul.1386, f32[2048]{0:T(1024)S(1)} %mul.1387, f32[2048]{0:T(1024)S(1)} %mul.1388, f32[2048]{0:T(1024)S(1)} %mul.1389, f32[2048]{0:T(1024)S(1)} %mul.1390, f32[2048]{0:T(1024)S(1)} %mul.1391, f32[2048]{0:T(1024)S(1)} %mul.1392, ...), kind=kLoop, calls=%fused_computation.48.clone.1 | loop fusion | flops 17039360 | bytes 10618945 | tf_op jit(solution)/shard_map/while/body/eval_jaxpr/add | solution.py:70
  243.6 6.9 %bitcast_reduce_fusion.17 = (bf16[128,128]{0,1:T(8,128)(2,1)S(1)}, bf16[128,128]{0,1:T(8,128)(2,1)S(1)}, bf16[128,128]{0,1:T(8,128)(2,1)S(1)}, bf16[128,128]{0,1...) fusion(f32[128,2048]{0,1:T(8,128)S(1)} %get-tuple-element.1035,, ...), kind=kLoop, calls=%fused_computation.64.clone.1 | loop fusion | flops 12320768 | bytes 9961536 | tf_op jit(solution)/shard_map/while/body/eval_jaxpr/reduce_sum | solution.py:71
  255.0 9.6 %fusion.126 = f32[128,2048]{0,1:T(8,128)S(1)} fusion(f32[128,2048]{0,1:T(8,128)S(1)} %get-tuple-element.987, f32[2048]{0:T(1024)S(1)} %mul.1386, f32[2048]{0:T(1024)S(1)} %mul.1387, f32[2048]{0:T(1024)S(1)} %mul.1388, f32[2048]{0:T(1024)S(1)} %mul.1389, f32[2048]{0:T(1024)S(1)} %mul.1390, f32[2048]{0:T(1024)S(1)} %mul.1391, f32[2048]{0:T(1024)S(1)} %mul.1392, ...), kind=kLoop, calls=%fused_computation.48.clone.1 | loop fusion | flops 17039360 | bytes 10618945 | tf_op jit(solution)/shard_map/while/body/eval_jaxpr/add | solution.py:70
  266.0 6.9 %bitcast_reduce_fusion.17 = (bf16[128,128]{0,1:T(8,128)(2,1)S(1)}, bf16[128,128]{0,1:T(8,128)(2,1)S(1)}, bf16[128,128]{0,1:T(8,128)(2,1)S(1)}, bf16[128,128]{0,1...) fusion(f32[128,2048]{0,1:T(8,128)S(1)} %get-tuple-element.1035,, ...), kind=kLoop, calls=%fused_computation.64.clone.1 | loop fusion | flops 12320768 | bytes 9961536 | tf_op jit(solution)/shard_map/while/body/eval_jaxpr/reduce_sum | solution.py:71
  277.3 9.6 %fusion.126 = f32[128,2048]{0,1:T(8,128)S(1)} fusion(f32[128,2048]{0,1:T(8,128)S(1)} %get-tuple-element.987, f32[2048]{0:T(1024)S(1)} %mul.1386, f32[2048]{0:T(1024)S(1)} %mul.1387, f32[2048]{0:T(1024)S(1)} %mul.1388, f32[2048]{0:T(1024)S(1)} %mul.1389, f32[2048]{0:T(1024)S(1)} %mul.1390, f32[2048]{0:T(1024)S(1)} %mul.1391, f32[2048]{0:T(1024)S(1)} %mul.1392, ...), kind=kLoop, calls=%fused_computation.48.clone.1 | loop fusion | flops 17039360 | bytes 10618945 | tf_op jit(solution)/shard_map/while/body/eval_jaxpr/add | solution.py:70
  288.3 6.9 %bitcast_reduce_fusion.17 = (bf16[128,128]{0,1:T(8,128)(2,1)S(1)}, bf16[128,128]{0,1:T(8,128)(2,1)S(1)}, bf16[128,128]{0,1:T(8,128)(2,1)S(1)}, bf16[128,128]{0,1...) fusion(f32[128,2048]{0,1:T(8,128)S(1)} %get-tuple-element.1035,, ...), kind=kLoop, calls=%fused_computation.64.clone.1 | loop fusion | flops 12320768 | bytes 9961536 | tf_op jit(solution)/shard_map/while/body/eval_jaxpr/reduce_sum | solution.py:71
  299.6 9.6 %fusion.126 = f32[128,2048]{0,1:T(8,128)S(1)} fusion(f32[128,2048]{0,1:T(8,128)S(1)} %get-tuple-element.987, f32[2048]{0:T(1024)S(1)} %mul.1386, f32[2048]{0:T(1024)S(1)} %mul.1387, f32[2048]{0:T(1024)S(1)} %mul.1388, f32[2048]{0:T(1024)S(1)} %mul.1389, f32[2048]{0:T(1024)S(1)} %mul.1390, f32[2048]{0:T(1024)S(1)} %mul.1391, f32[2048]{0:T(1024)S(1)} %mul.1392, ...), kind=kLoop, calls=%fused_computation.48.clone.1 | loop fusion | flops 17039360 | bytes 10618945 | tf_op jit(solution)/shard_map/while/body/eval_jaxpr/add | solution.py:70
  309.6 1.2 fusion.119
  311.0 1.9 collective-permute-start.3
  313.0 1.4 collective-permute-done.3
  314.6 2.6 fusion.111
  317.2 85.1 %all-reduce.2.cloned.1.call-done = f32[128,128]{1,0:T(8,128)} async-done(((f32[128,128]{1,0:T(8,128)}), f32[128,128]{1,0:T(8,128)}) %all-reduce.2.cloned.1.call-update) | async-done | bytes 65552 | tf_op jit(solution)/shard_map/psum | solution.py:103
  402.2 1.5 multiply_bitcast_fusion
  (681 shorter events, 67.4 us)
Async XLA Ops:
  7.2 395.1 %all-reduce.2.cloned.1.call-start = ((), (), s32[]{:S(2)}) async-start(), calls=%async_computation | async-start | bytes 131072 | tf_op jit(solution)/shard_map/psum | solution.py:103
  7.2 24.1 %copy-start.5 = (bf16[1,128,128]{2,1,0:T(8,128)(2,1)S(1)}, bf16[1,128,128]{2,1,0:T(8,128)(2,1)}, u32[]{:S(2)}) copy-start(bf16[1,128,128]{2,1,0:T(8,128)(2,1)} %param.11) | copy-start | bytes 98308
  7.2 13.9 %collective-permute-start = (bf16[128,2048]{1,0:T(8,128)(2,1)}, bf16[128,2048]{1,0:T(8,128)(2,1)S(1)}, u32[]{:S(2)}, u32[]{:S(2)}) collective-permute-start(bf16[128,2048]{1,0:T(8,128)(2,1)} %bitcast.309), channel_id=1, source_target_pairs={{0,16},{16,0},{1,17},{17,1},{2,18},{18,2},{3,19},{19,3},{4,20},{20... | collective-permute-start | bytes 1572872 | tf_op jit(solution)/shard_map/ppermute | solution.py:10
  21.2 3.4 copy-start.4
  22.6 8.7 %copy-start.2 = (bf16[128,2048]{1,0:T(8,128)(2,1)}, bf16[128,2048]{1,0:T(8,128)(2,1)S(1)}, u32[]{:S(2)}) copy-start(bf16[128,2048]{1,0:T(8,128)(2,1)S(1)} %fusion.112) | copy-start | bytes 1572868
  22.6 8.6 %collective-permute-start.2 = (bf16[128,2048]{1,0:T(8,128)(2,1)S(1)}, bf16[128,2048]{1,0:T(8,128)(2,1)S(1)}, u32[]{:S(2)}, u32[]{:S(2)}) collective-permute-start(bf16[128,2048]{1,0:T(8,128)(2,1)S(1)} %fusion.112), channel_id=1, source_target_pairs={{1,0},{2,1},{3,2},{4,3},{5,4},{6,5},{7,6},{8,7},{9,8},{10,9},{11,1... | collective-permute-start | bytes 1572872 | tf_op jit(solution)/shard_map/ppermute | solution.py:16
  112.7 6.4 %copy-start.6 = (bf16[1,3,3,2048]{3,2,1,0:T(4,128)(2,1)S(1)}, bf16[1,3,3,2048]{3,2,1,0:T(4,128)(2,1)}, u32[]{:S(2)}) copy-start(bf16[1,3,3,2048]{3,2,1,0:T(4,128)(2,1)} %param.12) | copy-start | bytes 110596
  112.7 6.6 %copy-start.3 = (bf16[128,2048]{1,0:T(8,128)(2,1)S(1)}, bf16[128,2048]{1,0:T(8,128)(2,1)}, u32[]{:S(2)}) copy-start(bf16[128,2048]{1,0:T(8,128)(2,1)} %copy-done.2) | copy-start | bytes 1572868
  115.3 11.7 %collective-permute-start.1 = (bf16[128,2048]{1,0:T(8,128)(2,1)S(1)}, bf16[128,2048]{1,0:T(8,128)(2,1)}, u32[]{:S(2)}, u32[]{:S(2)}) collective-permute-start(bf16[128,2048]{1,0:T(8,128)(2,1)S(1)} %get-tuple-element.492), channel_id=1, source_target_pairs={{0,1},{1,2},{2,3},{3,4},{4,5},{5,6},{6,7},{7,8},{8,9},{9,10},{10,1... | collective-permute-start | bytes 1572872 | tf_op jit(solution)/shard_map/ppermute | solution.py:16
  309.2 1.5 copy-start
  309.2 1.5 copy-start.1
  311.0 3.4 collective-permute-start.3
Sparse Core Ops, SparseCore 0:
  313.2 89.0 all-reduce.1
where the time goes:
time: 411 us
  other arithmetic  200 us (49%)
  waiting for transfers between devices  111 us (27%)
  local copies, waits for them, and re-layouts  61.2 us (15%)
  between operations  14.3 us (3%)
  loops' own time  14.2 us (3%)
  starting transfers between devices  9.31 us (2%)
    psum x1, waiting for transfers between devices, body(): summed = lax.psum(filter_sum, 'ctx')  85.1 us
    add x8, other arithmetic, forward_step(): total = total + jnp.where(usable, shifted * weights[None, :], 0.0)  76.8 us
    reduce_sum x8, other arithmetic, forward_step(): jnp.sum((grad_wide * shifted).reshape(row_count, groups, members), axis=2)  55.5 us
    add x8, other arithmetic, step(): total + jnp.where((lag <= ahead_pos)[:, None], ahead * weights[None, :],...  44.8 us
    ppermute x3, waiting for transfers between devices, shifted_2(): return lax.ppermute(block, axis, route)  13.8 us
    ppermute x1, waiting for transfers between devices, from_behind(): lax.ppermute(shard, axis, [(i, (i + by) % count) for i in range(count)])  12.4 us
    mul x128, local copies, waits for them, and re-layouts, step(): ahead * weights[None, :]  12.2 us
    mul x128, local copies, waits for them, and re-layouts, forward_step(): total = total + jnp.where(usable, shifted * weights[None, :], 0.0)  12.2 us
  transfers between devices with their start and end apart: 5, of which 5 were waited for; matrix products, arithmetic and copies ran while one was open for 1% of the time, Pallas kernels for 0%

commit v1 on v0

--- a/solution.py
+++ b/solution.py
@@ -100,7 +100,12 @@
             0.0,
         )
     grad_pre = total.astype(jnp.bfloat16)[None]
-    summed = lax.psum(filter_sum, "ctx")
+
+    def _lift_shelves(field_in):
+        r_now = jnp.sum(lax.all_gather(field_in, "ctx"), 0)
+        return r_now
+
+    summed = _lift_shelves(filter_sum)
     filter_grad = (summed / math.sqrt(row_count * devices * members))[None]
     return (grad_pre, filter_grad)
 

time: 411 us -> 358 us (0.87)
  waiting for transfers between devices: 111 us -> 55.6 us
    psum x1 -> x0, waiting for transfers between devices: 85.1 us -> none  [body(): summed = lax.psum(filter_sum, 'ctx')]
    all_gather x0 -> x1, waiting for transfers between devices: none -> 29.3 us  [_lift_shelves(): r_now = jnp.sum(lax.all_gather(field_in, 'ctx'), 0)]
  transfers between devices with their start and end apart: 5 -> 5, of which waited for: 5 -> 5; matrix products, arithmetic and copies ran while one was open for 1% -> 2% of each run, Pallas kernels for 0% -> 0%
where the time goes in v1:
time: 358 us; the launch traced here: 355 us
  other arithmetic  200 us (56%)
  local copies, waits for them, and re-layouts  61.2 us (17%)
  waiting for transfers between devices  55.6 us (16%)
  between operations  14.3 us (4%)
  loops' own time  14.2 us (4%)
  starting transfers between devices  9.31 us (3%)
    add x8, other arithmetic, forward_step(): total = total + jnp.where(usable, shifted * weights[None, :], 0.0)  76.4 us
    reduce_sum x8, other arithmetic, forward_step(): jnp.sum((grad_wide * shifted).reshape(row_count, groups, members), axis=2)  55 us
    add x8, other arithmetic, step(): total + jnp.where((lag <= ahead_pos)[:, None], ahead * weights[None, :],...  44.8 us
    all_gather x1, waiting for transfers between devices, _lift_shelves(): r_now = jnp.sum(lax.all_gather(field_in, 'ctx'), 0)  29.3 us
    ppermute x3, waiting for transfers between devices, shifted_2(): return lax.ppermute(block, axis, route)  13.9 us
    ppermute x1, waiting for transfers between devices, from_behind(): lax.ppermute(shard, axis, [(i, (i + by) % count) for i in range(count)])  12.4 us
    mul x128, local copies, waits for them, and re-layouts, forward_step(): total = total + jnp.where(usable, shifted * weights[None, :], 0.0)  12.2 us
    mul x128, local copies, waits for them, and re-layouts, step(): ahead * weights[None, :]  12.2 us
  transfers between devices with their start and end apart: 5, of which 5 were waited for; matrix products, arithmetic and copies ran while one was open for 2% of the time, Pallas kernels for 0%

profile of v1, /device:TPU:8, one launch (start us, length us, event | category | flops | bytes accessed | tf_op | source)
XLA Modules:
  0.0 354.5 jit_solution(16049538584396699361)
XLA Ops:
  7.2 1.6 collective-permute-start
  8.8 12.4 %collective-permute-done = bf16[128,2048]{1,0:T(8,128)(2,1)S(1)} collective-permute-done((bf16[128,2048]{1,0:T(8,128)(2,1)}, bf16[128,2048]{1,0:T(8,128)(2,1)S(1)}, u32[]{:S(2)}, u32[]{:S(2)}) %collective-permute-start) | collective-permute-done | bytes 524320 | tf_op jit(solution)/shard_map/ppermute | solution.py:10
  21.2 1.4 fusion.112
  22.6 1.9 collective-permute-start.2
  24.5 0.7 copy.16
  26.2 5.0 %collective-permute-done.2 = bf16[128,2048]{1,0:T(8,128)(2,1)S(1)} collective-permute-done((bf16[128,2048]{1,0:T(8,128)(2,1)S(1)}, bf16[128,2048]{1,0:T(8,128)(2,1)S(1)}, u32[]{:S(2)}, u32[]{:S(2)}) %collective-permute-start.2) | collective-permute-done | bytes 524320 | tf_op jit(solution)/shard_map/ppermute | solution.py:16
  31.3 81.3 %while.30 = (s32[]{:T(128)}, f32[128,2048]{1,0:T(8,128)S(1)}, s32[8]{0:T(128)S(1)}, s32[256]{0:T(256)S(1)}, bf16[256,2048]{1,0:T(8,128)(2,1)S(1)}, /*index=5*/bf...) while((s32[]{:T(128)}, f32[128,2048]{1,0:T(8,128)S(1)}, ...), condition=%wide.region_37.38_spmd.clone, body=%wide.region_36.37_spmd.clone.sunk | while | flops 17043556 | bytes 11044691 | solution.py:33
  31.3 0.7 dynamic_slice.941
  35.9 5.6 %fusion.128 = f32[128,2048]{1,0:T(8,128)S(1)} fusion(f32[128,2048]{1,0:T(8,128)S(1)} %get-tuple-element.835, f32[2048]{0:T(1024)S(1)} %mul.1435, bf16[256,2048]{1,0:T(8,128)(2,1)S(1)} %get-tuple-element.893, s32[]{:T(128)S(6)} %select_n.1196, f32[2048]{0:T(1024)S(1)} %mul.1436, s32[]{:T(128)S(6)} %select_n.1197, f32[2048]{0:T(1024)S(1)} %mul.1437, ...), kind=kLoop, calls=%fused_computation.176.clone.1 | loop fusion | flops 17039360 | bytes 10618945 | tf_op jit(solution)/shard_map/while/body/eval_jaxpr/add | solution.py:29
  41.5 0.7 dynamic_slice.941
  46.0 5.6 %fusion.128 = f32[128,2048]{1,0:T(8,128)S(1)} fusion(f32[128,2048]{1,0:T(8,128)S(1)} %get-tuple-element.835, f32[2048]{0:T(1024)S(1)} %mul.1435, bf16[256,2048]{1,0:T(8,128)(2,1)S(1)} %get-tuple-element.893, s32[]{:T(128)S(6)} %select_n.1196, f32[2048]{0:T(1024)S(1)} %mul.1436, s32[]{:T(128)S(6)} %select_n.1197, f32[2048]{0:T(1024)S(1)} %mul.1437, ...), kind=kLoop, calls=%fused_computation.176.clone.1 | loop fusion | flops 17039360 | bytes 10618945 | tf_op jit(solution)/shard_map/while/body/eval_jaxpr/add | solution.py:29
  51.7 0.7 dynamic_slice.941
  56.2 5.6 %fusion.128 = f32[128,2048]{1,0:T(8,128)S(1)} fusion(f32[128,2048]{1,0:T(8,128)S(1)} %get-tuple-element.835, f32[2048]{0:T(1024)S(1)} %mul.1435, bf16[256,2048]{1,0:T(8,128)(2,1)S(1)} %get-tuple-element.893, s32[]{:T(128)S(6)} %select_n.1196, f32[2048]{0:T(1024)S(1)} %mul.1436, s32[]{:T(128)S(6)} %select_n.1197, f32[2048]{0:T(1024)S(1)} %mul.1437, ...), kind=kLoop, calls=%fused_computation.176.clone.1 | loop fusion | flops 17039360 | bytes 10618945 | tf_op jit(solution)/shard_map/while/body/eval_jaxpr/add | solution.py:29
  61.8 0.7 dynamic_slice.941
  66.4 5.6 %fusion.128 = f32[128,2048]{1,0:T(8,128)S(1)} fusion(f32[128,2048]{1,0:T(8,128)S(1)} %get-tuple-element.835, f32[2048]{0:T(1024)S(1)} %mul.1435, bf16[256,2048]{1,0:T(8,128)(2,1)S(1)} %get-tuple-element.893, s32[]{:T(128)S(6)} %select_n.1196, f32[2048]{0:T(1024)S(1)} %mul.1436, s32[]{:T(128)S(6)} %select_n.1197, f32[2048]{0:T(1024)S(1)} %mul.1437, ...), kind=kLoop, calls=%fused_computation.176.clone.1 | loop fusion | flops 17039360 | bytes 10618945 | tf_op jit(solution)/shard_map/while/body/eval_jaxpr/add | solution.py:29
  72.0 0.7 dynamic_slice.941
  76.5 5.6 %fusion.128 = f32[128,2048]{1,0:T(8,128)S(1)} fusion(f32[128,2048]{1,0:T(8,128)S(1)} %get-tuple-element.835, f32[2048]{0:T(1024)S(1)} %mul.1435, bf16[256,2048]{1,0:T(8,128)(2,1)S(1)} %get-tuple-element.893, s32[]{:T(128)S(6)} %select_n.1196, f32[2048]{0:T(1024)S(1)} %mul.1436, s32[]{:T(128)S(6)} %select_n.1197, f32[2048]{0:T(1024)S(1)} %mul.1437, ...), kind=kLoop, calls=%fused_computation.176.clone.1 | loop fusion | flops 17039360 | bytes 10618945 | tf_op jit(solution)/shard_map/while/body/eval_jaxpr/add | solution.py:29
  86.7 5.6 %fusion.128 = f32[128,2048]{1,0:T(8,128)S(1)} fusion(f32[128,2048]{1,0:T(8,128)S(1)} %get-tuple-element.835, f32[2048]{0:T(1024)S(1)} %mul.1435, bf16[256,2048]{1,0:T(8,128)(2,1)S(1)} %get-tuple-element.893, s32[]{:T(128)S(6)} %select_n.1196, f32[2048]{0:T(1024)S(1)} %mul.1436, s32[]{:T(128)S(6)} %select_n.1197, f32[2048]{0:T(1024)S(1)} %mul.1437, ...), kind=kLoop, calls=%fused_computation.176.clone.1 | loop fusion | flops 17039360 | bytes 10618945 | tf_op jit(solution)/shard_map/while/body/eval_jaxpr/add | solution.py:29
  96.9 5.6 %fusion.128 = f32[128,2048]{1,0:T(8,128)S(1)} fusion(f32[128,2048]{1,0:T(8,128)S(1)} %get-tuple-element.835, f32[2048]{0:T(1024)S(1)} %mul.1435, bf16[256,2048]{1,0:T(8,128)(2,1)S(1)} %get-tuple-element.893, s32[]{:T(128)S(6)} %select_n.1196, f32[2048]{0:T(1024)S(1)} %mul.1436, s32[]{:T(128)S(6)} %select_n.1197, f32[2048]{0:T(1024)S(1)} %mul.1437, ...), kind=kLoop, calls=%fused_computation.176.clone.1 | loop fusion | flops 17039360 | bytes 10618945 | tf_op jit(solution)/shard_map/while/body/eval_jaxpr/add | solution.py:29
  107.0 5.6 %fusion.128 = f32[128,2048]{1,0:T(8,128)S(1)} fusion(f32[128,2048]{1,0:T(8,128)S(1)} %get-tuple-element.835, f32[2048]{0:T(1024)S(1)} %mul.1435, bf16[256,2048]{1,0:T(8,128)(2,1)S(1)} %get-tuple-element.893, s32[]{:T(128)S(6)} %select_n.1196, f32[2048]{0:T(1024)S(1)} %mul.1436, s32[]{:T(128)S(6)} %select_n.1197, f32[2048]{0:T(1024)S(1)} %mul.1437, ...), kind=kLoop, calls=%fused_computation.176.clone.1 | loop fusion | flops 17039360 | bytes 10618945 | tf_op jit(solution)/shard_map/while/body/eval_jaxpr/add | solution.py:29
  112.7 2.6 fusion.118
  115.3 3.8 %collective-permute-start.1 = (bf16[128,2048]{1,0:T(8,128)(2,1)S(1)}, bf16[128,2048]{1,0:T(8,128)(2,1)}, u32[]{:S(2)}, u32[]{:S(2)}) collective-permute-start(bf16[128,2048]{1,0:T(8,128)(2,1)S(1)} %get-tuple-element.492), channel_id=1, source_target_pairs={{0,1},{1,2},{2,3},{3,4},{4,5},{5,6},{6,7},{7,8},{8,9},{9,10},{10,1... | collective-permute-start | bytes 1572872 | tf_op jit(solution)/shard_map/ppermute | solution.py:16
  119.4 7.5 %collective-permute-done.1 = bf16[128,2048]{1,0:T(8,128)(2,1)} collective-permute-done((bf16[128,2048]{1,0:T(8,128)(2,1)S(1)}, bf16[128,2048]{1,0:T(8,128)(2,1)}, u32[]{:S(2)}, u32[]{:S(2)}) %collective-permute-start.1) | collective-permute-done | bytes 524320 | tf_op jit(solution)/shard_map/ppermute | solution.py:16
  126.9 2.2 pad_maximum_fusion.2
  129.1 1.5 copy.17
  130.6 177.8 %while.29 = (s32[]{:T(128)}, f32[128,2048]{0,1:T(8,128)S(1)}, f32[8,16,128]{2,1,0:T(8,128)}, s32[8]{0:T(128)S(1)}, s32[128]{0:T(128)S(1)}, /*index=5*/bf16[256,2...) while((s32[]{:T(128)}, f32[128,2048]{0,1:T(8,128)S(1)}, ...), condition=%wide.region_35.36_spmd.clone, body=%wide.region_2.35_spmd.clone.sunk | while | flops 30148740 | bytes 21566524 | solution.py:79
  132.0 6.9 %bitcast_reduce_fusion.17 = (bf16[128,128]{0,1:T(8,128)(2,1)S(1)}, bf16[128,128]{0,1:T(8,128)(2,1)S(1)}, bf16[128,128]{0,1:T(8,128)(2,1)S(1)}, bf16[128,128]{0,1...) fusion(f32[128,2048]{0,1:T(8,128)S(1)} %get-tuple-element.1035,, ...), kind=kLoop, calls=%fused_computation.64.clone.1 | loop fusion | flops 12320768 | bytes 9961536 | tf_op jit(solution)/shard_map/while/body/eval_jaxpr/reduce_sum | solution.py:71
  143.3 9.6 %fusion.126 = f32[128,2048]{0,1:T(8,128)S(1)} fusion(f32[128,2048]{0,1:T(8,128)S(1)} %get-tuple-element.987, f32[2048]{0:T(1024)S(1)} %mul.1386, f32[2048]{0:T(1024)S(1)} %mul.1387, f32[2048]{0:T(1024)S(1)} %mul.1388, f32[2048]{0:T(1024)S(1)} %mul.1389, f32[2048]{0:T(1024)S(1)} %mul.1390, f32[2048]{0:T(1024)S(1)} %mul.1391, f32[2048]{0:T(1024)S(1)} %mul.1392, ...), kind=kLoop, calls=%fused_computation.48.clone.1 | loop fusion | flops 17039360 | bytes 10618945 | tf_op jit(solution)/shard_map/while/body/eval_jaxpr/add | solution.py:70
  154.2 6.9 %bitcast_reduce_fusion.17 = (bf16[128,128]{0,1:T(8,128)(2,1)S(1)}, bf16[128,128]{0,1:T(8,128)(2,1)S(1)}, bf16[128,128]{0,1:T(8,128)(2,1)S(1)}, bf16[128,128]{0,1...) fusion(f32[128,2048]{0,1:T(8,128)S(1)} %get-tuple-element.1035,, ...), kind=kLoop, calls=%fused_computation.64.clone.1 | loop fusion | flops 12320768 | bytes 9961536 | tf_op jit(solution)/shard_map/while/body/eval_jaxpr/reduce_sum | solution.py:71
  165.5 9.6 %fusion.126 = f32[128,2048]{0,1:T(8,128)S(1)} fusion(f32[128,2048]{0,1:T(8,128)S(1)} %get-tuple-element.987, f32[2048]{0:T(1024)S(1)} %mul.1386, f32[2048]{0:T(1024)S(1)} %mul.1387, f32[2048]{0:T(1024)S(1)} %mul.1388, f32[2048]{0:T(1024)S(1)} %mul.1389, f32[2048]{0:T(1024)S(1)} %mul.1390, f32[2048]{0:T(1024)S(1)} %mul.1391, f32[2048]{0:T(1024)S(1)} %mul.1392, ...), kind=kLoop, calls=%fused_computation.48.clone.1 | loop fusion | flops 17039360 | bytes 10618945 | tf_op jit(solution)/shard_map/while/body/eval_jaxpr/add | solution.py:70
  176.5 6.9 %bitcast_reduce_fusion.17 = (bf16[128,128]{0,1:T(8,128)(2,1)S(1)}, bf16[128,128]{0,1:T(8,128)(2,1)S(1)}, bf16[128,128]{0,1:T(8,128)(2,1)S(1)}, bf16[128,128]{0,1...) fusion(f32[128,2048]{0,1:T(8,128)S(1)} %get-tuple-element.1035,, ...), kind=kLoop, calls=%fused_computation.64.clone.1 | loop fusion | flops 12320768 | bytes 9961536 | tf_op jit(solution)/shard_map/while/body/eval_jaxpr/reduce_sum | solution.py:71
  187.7 9.6 %fusion.126 = f32[128,2048]{0,1:T(8,128)S(1)} fusion(f32[128,2048]{0,1:T(8,128)S(1)} %get-tuple-element.987, f32[2048]{0:T(1024)S(1)} %mul.1386, f32[2048]{0:T(1024)S(1)} %mul.1387, f32[2048]{0:T(1024)S(1)} %mul.1388, f32[2048]{0:T(1024)S(1)} %mul.1389, f32[2048]{0:T(1024)S(1)} %mul.1390, f32[2048]{0:T(1024)S(1)} %mul.1391, f32[2048]{0:T(1024)S(1)} %mul.1392, ...), kind=kLoop, calls=%fused_computation.48.clone.1 | loop fusion | flops 17039360 | bytes 10618945 | tf_op jit(solution)/shard_map/while/body/eval_jaxpr/add | solution.py:70
  198.7 6.9 %bitcast_reduce_fusion.17 = (bf16[128,128]{0,1:T(8,128)(2,1)S(1)}, bf16[128,128]{0,1:T(8,128)(2,1)S(1)}, bf16[128,128]{0,1:T(8,128)(2,1)S(1)}, bf16[128,128]{0,1...) fusion(f32[128,2048]{0,1:T(8,128)S(1)} %get-tuple-element.1035,, ...), kind=kLoop, calls=%fused_computation.64.clone.1 | loop fusion | flops 12320768 | bytes 9961536 | tf_op jit(solution)/shard_map/while/body/eval_jaxpr/reduce_sum | solution.py:71
  210.0 9.6 %fusion.126 = f32[128,2048]{0,1:T(8,128)S(1)} fusion(f32[128,2048]{0,1:T(8,128)S(1)} %get-tuple-element.987, f32[2048]{0:T(1024)S(1)} %mul.1386, f32[2048]{0:T(1024)S(1)} %mul.1387, f32[2048]{0:T(1024)S(1)} %mul.1388, f32[2048]{0:T(1024)S(1)} %mul.1389, f32[2048]{0:T(1024)S(1)} %mul.1390, f32[2048]{0:T(1024)S(1)} %mul.1391, f32[2048]{0:T(1024)S(1)} %mul.1392, ...), kind=kLoop, calls=%fused_computation.48.clone.1 | loop fusion | flops 17039360 | bytes 10618945 | tf_op jit(solution)/shard_map/while/body/eval_jaxpr/add | solution.py:70
  220.9 6.9 %bitcast_reduce_fusion.17 = (bf16[128,128]{0,1:T(8,128)(2,1)S(1)}, bf16[128,128]{0,1:T(8,128)(2,1)S(1)}, bf16[128,128]{0,1:T(8,128)(2,1)S(1)}, bf16[128,128]{0,1...) fusion(f32[128,2048]{0,1:T(8,128)S(1)} %get-tuple-element.1035,, ...), kind=kLoop, calls=%fused_computation.64.clone.1 | loop fusion | flops 12320768 | bytes 9961536 | tf_op jit(solution)/shard_map/while/body/eval_jaxpr/reduce_sum | solution.py:71
  232.2 9.6 %fusion.126 = f32[128,2048]{0,1:T(8,128)S(1)} fusion(f32[128,2048]{0,1:T(8,128)S(1)} %get-tuple-element.987, f32[2048]{0:T(1024)S(1)} %mul.1386, f32[2048]{0:T(1024)S(1)} %mul.1387, f32[2048]{0:T(1024)S(1)} %mul.1388, f32[2048]{0:T(1024)S(1)} %mul.1389, f32[2048]{0:T(1024)S(1)} %mul.1390, f32[2048]{0:T(1024)S(1)} %mul.1391, f32[2048]{0:T(1024)S(1)} %mul.1392, ...), kind=kLoop, calls=%fused_computation.48.clone.1 | loop fusion | flops 17039360 | bytes 10618945 | tf_op jit(solution)/shard_map/while/body/eval_jaxpr/add | solution.py:70
  243.1 6.9 %bitcast_reduce_fusion.17 = (bf16[128,128]{0,1:T(8,128)(2,1)S(1)}, bf16[128,128]{0,1:T(8,128)(2,1)S(1)}, bf16[128,128]{0,1:T(8,128)(2,1)S(1)}, bf16[128,128]{0,1...) fusion(f32[128,2048]{0,1:T(8,128)S(1)} %get-tuple-element.1035,, ...), kind=kLoop, calls=%fused_computation.64.clone.1 | loop fusion | flops 12320768 | bytes 9961536 | tf_op jit(solution)/shard_map/while/body/eval_jaxpr/reduce_sum | solution.py:71
  254.4 9.6 %fusion.126 = f32[128,2048]{0,1:T(8,128)S(1)} fusion(f32[128,2048]{0,1:T(8,128)S(1)} %get-tuple-element.987, f32[2048]{0:T(1024)S(1)} %mul.1386, f32[2048]{0:T(1024)S(1)} %mul.1387, f32[2048]{0:T(1024)S(1)} %mul.1388, f32[2048]{0:T(1024)S(1)} %mul.1389, f32[2048]{0:T(1024)S(1)} %mul.1390, f32[2048]{0:T(1024)S(1)} %mul.1391, f32[2048]{0:T(1024)S(1)} %mul.1392, ...), kind=kLoop, calls=%fused_computation.48.clone.1 | loop fusion | flops 17039360 | bytes 10618945 | tf_op jit(solution)/shard_map/while/body/eval_jaxpr/add | solution.py:70
  265.4 6.9 %bitcast_reduce_fusion.17 = (bf16[128,128]{0,1:T(8,128)(2,1)S(1)}, bf16[128,128]{0,1:T(8,128)(2,1)S(1)}, bf16[128,128]{0,1:T(8,128)(2,1)S(1)}, bf16[128,128]{0,1...) fusion(f32[128,2048]{0,1:T(8,128)S(1)} %get-tuple-element.1035,, ...), kind=kLoop, calls=%fused_computation.64.clone.1 | loop fusion | flops 12320768 | bytes 9961536 | tf_op jit(solution)/shard_map/while/body/eval_jaxpr/reduce_sum | solution.py:71
  276.6 9.6 %fusion.126 = f32[128,2048]{0,1:T(8,128)S(1)} fusion(f32[128,2048]{0,1:T(8,128)S(1)} %get-tuple-element.987, f32[2048]{0:T(1024)S(1)} %mul.1386, f32[2048]{0:T(1024)S(1)} %mul.1387, f32[2048]{0:T(1024)S(1)} %mul.1388, f32[2048]{0:T(1024)S(1)} %mul.1389, f32[2048]{0:T(1024)S(1)} %mul.1390, f32[2048]{0:T(1024)S(1)} %mul.1391, f32[2048]{0:T(1024)S(1)} %mul.1392, ...), kind=kLoop, calls=%fused_computation.48.clone.1 | loop fusion | flops 17039360 | bytes 10618945 | tf_op jit(solution)/shard_map/while/body/eval_jaxpr/add | solution.py:70
  287.6 6.9 %bitcast_reduce_fusion.17 = (bf16[128,128]{0,1:T(8,128)(2,1)S(1)}, bf16[128,128]{0,1:T(8,128)(2,1)S(1)}, bf16[128,128]{0,1:T(8,128)(2,1)S(1)}, bf16[128,128]{0,1...) fusion(f32[128,2048]{0,1:T(8,128)S(1)} %get-tuple-element.1035,, ...), kind=kLoop, calls=%fused_computation.64.clone.1 | loop fusion | flops 12320768 | bytes 9961536 | tf_op jit(solution)/shard_map/while/body/eval_jaxpr/reduce_sum | solution.py:71
  298.9 9.6 %fusion.126 = f32[128,2048]{0,1:T(8,128)S(1)} fusion(f32[128,2048]{0,1:T(8,128)S(1)} %get-tuple-element.987, f32[2048]{0:T(1024)S(1)} %mul.1386, f32[2048]{0:T(1024)S(1)} %mul.1387, f32[2048]{0:T(1024)S(1)} %mul.1388, f32[2048]{0:T(1024)S(1)} %mul.1389, f32[2048]{0:T(1024)S(1)} %mul.1390, f32[2048]{0:T(1024)S(1)} %mul.1391, f32[2048]{0:T(1024)S(1)} %mul.1392, ...), kind=kLoop, calls=%fused_computation.48.clone.1 | loop fusion | flops 17039360 | bytes 10618945 | tf_op jit(solution)/shard_map/while/body/eval_jaxpr/add | solution.py:70
  308.9 1.2 fusion.119
  310.3 1.9 collective-permute-start.3
  312.3 1.4 collective-permute-done.3
  313.8 2.6 fusion.111
  316.4 29.3 %all-gather.2.cloned.1.call-done = f32[16,128,128]{2,1,0:T(8,128)} async-done(((f32[1,128,128]{2,1,0:T(8,128)}), f32[16,128,128]{2,1,0:T(8,128)}) %all-gather.2.cloned.1.call-update) | async-done | bytes 1048592 | tf_op jit(solution)/shard_map/all_gather | solution.py:105
  345.7 1.3 reduce_sum.425
  (682 shorter events, 68.1 us)
Async XLA Ops:
  7.2 338.6 %all-gather.2.cloned.1.call-start = ((), (), s32[]{:S(2)}) async-start(), calls=%async_computation | async-start | bytes 1114112 | tf_op jit(solution)/shard_map/all_gather | solution.py:105
  7.2 24.1 %copy-start.5 = (bf16[1,128,128]{2,1,0:T(8,128)(2,1)S(1)}, bf16[1,128,128]{2,1,0:T(8,128)(2,1)}, u32[]{:S(2)}) copy-start(bf16[1,128,128]{2,1,0:T(8,128)(2,1)} %param.11) | copy-start | bytes 98308
  7.2 13.9 %collective-permute-start = (bf16[128,2048]{1,0:T(8,128)(2,1)}, bf16[128,2048]{1,0:T(8,128)(2,1)S(1)}, u32[]{:S(2)}, u32[]{:S(2)}) collective-permute-start(bf16[128,2048]{1,0:T(8,128)(2,1)} %bitcast.309), channel_id=1, source_target_pairs={{0,16},{16,0},{1,17},{17,1},{2,18},{18,2},{3,19},{19,3},{4,20},{20... | collective-permute-start | bytes 1572872 | tf_op jit(solution)/shard_map/ppermute | solution.py:10
  21.2 3.4 copy-start.4
  22.6 8.7 %copy-start.2 = (bf16[128,2048]{1,0:T(8,128)(2,1)}, bf16[128,2048]{1,0:T(8,128)(2,1)S(1)}, u32[]{:S(2)}) copy-start(bf16[128,2048]{1,0:T(8,128)(2,1)S(1)} %fusion.112) | copy-start | bytes 1572868
  22.6 8.6 %collective-permute-start.2 = (bf16[128,2048]{1,0:T(8,128)(2,1)S(1)}, bf16[128,2048]{1,0:T(8,128)(2,1)S(1)}, u32[]{:S(2)}, u32[]{:S(2)}) collective-permute-start(bf16[128,2048]{1,0:T(8,128)(2,1)S(1)} %fusion.112), channel_id=1, source_target_pairs={{1,0},{2,1},{3,2},{4,3},{5,4},{6,5},{7,6},{8,7},{9,8},{10,9},{11,1... | collective-permute-start | bytes 1572872 | tf_op jit(solution)/shard_map/ppermute | solution.py:16
  112.7 6.5 %copy-start.6 = (bf16[1,3,3,2048]{3,2,1,0:T(4,128)(2,1)S(1)}, bf16[1,3,3,2048]{3,2,1,0:T(4,128)(2,1)}, u32[]{:S(2)}) copy-start(bf16[1,3,3,2048]{3,2,1,0:T(4,128)(2,1)} %param.12) | copy-start | bytes 110596
  112.7 6.6 %copy-start.3 = (bf16[128,2048]{1,0:T(8,128)(2,1)S(1)}, bf16[128,2048]{1,0:T(8,128)(2,1)}, u32[]{:S(2)}) copy-start(bf16[128,2048]{1,0:T(8,128)(2,1)} %copy-done.2) | copy-start | bytes 1572868
  115.3 11.7 %collective-permute-start.1 = (bf16[128,2048]{1,0:T(8,128)(2,1)S(1)}, bf16[128,2048]{1,0:T(8,128)(2,1)}, u32[]{:S(2)}, u32[]{:S(2)}) collective-permute-start(bf16[128,2048]{1,0:T(8,128)(2,1)S(1)} %get-tuple-element.492), channel_id=1, source_target_pairs={{0,1},{1,2},{2,3},{3,4},{4,5},{5,6},{6,7},{7,8},{8,9},{9,10},{10,1... | collective-permute-start | bytes 1572872 | tf_op jit(solution)/shard_map/ppermute | solution.py:16
  308.5 1.5 copy-start
  308.5 1.5 copy-start.1
  310.3 3.4 collective-permute-start.3
Sparse Core Ops, SparseCore 0:
  308.6 37.1 all-gather.1
